TPU v7x, 512 devices: a whole 4x8x8 slice. The times are simulated.
512 devices in a mesh: rep: 4 (over x), ep: 128 (over z, y, core).
Axes of the slice: x: 4, y: 8, z: 8, core: 2. Of those that a mesh axis runs over, the one named last changes fastest.
Arguments:
- tokens: bfloat16 [16384, 2048], P('ep', 'rep'), may hold values from -6 to 6
- out_grad: bfloat16 [16384, 2048], P('ep', 'rep'), may hold values from -6 to 6
- expert_ids: int32 [16384, 8], P('ep'), may hold values from 0 to 127, all different within a row; in each aligned block of 128 rows (0 to 127, 128 to 255, ...) at most 9 rows name the same one
- route_weight: bfloat16 [16384, 8], P('ep'), may hold values from 0.019897461 to 0.29882812
- w_gate: bfloat16 [128, 2048, 640], P('ep', 'rep'), may hold values from -0.125 to 0.125
- w_up: bfloat16 [128, 2048, 640], P('ep', 'rep'), may hold values from -0.125 to 0.125
- w_down: bfloat16 [128, 640, 2048], P('ep', None, 'rep'), may hold values from -0.25 to 0.25
Outputs:
- token_grad: bfloat16 [16384, 2048], P('ep', 'rep')
- grad_gate: bfloat16 [128, 2048, 640], P('ep', 'rep')
- grad_up: bfloat16 [128, 2048, 640], P('ep', 'rep')
- grad_down: bfloat16 [128, 640, 2048], P('ep', None, 'rep')
Inputs may be any that keep to these rules, and one draw needn't show every extreme that they name: `expert_ids`: each token picks 8 different experts. Among the 128 tokens of one index of ep no expert is picked by more than 9 tokens, and in every draw some expert is picked by exactly 9 tokens of some such index.
All inputs are finite; a program needn't handle non-finite values.
Results may differ from a plain program's by a relative error of at most 0.024.
Values may be sent and summed in bfloat16 or wider, within the bound.
No kernel may reach another device: no remote copies, remote signals or barrier semaphores. Data moves between devices by JAX's collectives and lax.ppermute only.
A program may use at most 64 MiB of HBM per device.

v0:
```python
import jax
import jax.numpy as jnp
from jax import lax
from jax.sharding import PartitionSpec as P

CAP = 9


def hidden_terms(pre_gate, pre_up, pre_back, weight):
    sigmoid_gate = jax.nn.sigmoid(pre_gate)
    silu_gate = pre_gate * sigmoid_gate
    d_hidden = weight[..., None] * pre_back
    hidden = (silu_gate * pre_up).astype(jnp.bfloat16)
    gate_delta = (
        d_hidden * pre_up * sigmoid_gate * (1.0 + pre_gate * (1.0 - sigmoid_gate))
    ).astype(jnp.bfloat16)
    up_delta = (d_hidden * silu_gate).astype(jnp.bfloat16)
    return (hidden, gate_delta, up_delta)


def body(tokens, out_grad, expert_ids, route_weight, w_gate, w_up, w_down):
    ep_ranks = lax.axis_size("ep")
    local_count = w_gate.shape[0]
    experts = local_count * ep_ranks
    quarter = tokens.shape[1]
    slot_rows = ep_ranks * CAP
    slot_total = experts * CAP
    expert_range = jnp.arange(experts, dtype=jnp.int32)
    matches = expert_ids[:, :, None] == expert_range[None, None, :]
    picked = jnp.sum(matches.astype(jnp.int32), axis=1)
    before = jnp.cumsum(picked, axis=0) - picked
    position = jnp.sum(jnp.where(matches, before[:, None, :], 0), axis=2)
    owner_col = expert_ids // local_count
    within = expert_ids % local_count
    slot_index = (within * ep_ranks + owner_col) * CAP + position
    select = slot_index[:, :, None] == jnp.arange(slot_total, dtype=jnp.int32)[None, None, :]
    placing = jnp.any(select, axis=1).astype(jnp.bfloat16)
    send_tokens = jnp.einsum("ts,td->sd", placing, tokens, preferred_element_type=jnp.float32)
    send_tokens = send_tokens.astype(jnp.bfloat16).reshape(local_count, ep_ranks, CAP, quarter)
    send_grads = jnp.einsum("ts,td->sd", placing, out_grad, preferred_element_type=jnp.float32)
    send_grads = send_grads.astype(jnp.bfloat16).reshape(local_count, ep_ranks, CAP, quarter)
    send_weight = jnp.sum(
        jnp.where(select, route_weight.astype(jnp.float32)[:, :, None], 0.0), axis=(0, 1)
    )
    send_weight = send_weight.astype(jnp.bfloat16).reshape(local_count, ep_ranks, CAP)
    routed_tokens, routed_grads, routed_weight = (
        lax.all_to_all(send_tokens, "ep", split_axis=1, concat_axis=1, tiled=True),
        lax.all_to_all(send_grads, "ep", split_axis=1, concat_axis=1, tiled=True),
        lax.all_to_all(send_weight, "ep", split_axis=1, concat_axis=1, tiled=True),
    )
    routed_tokens = routed_tokens.reshape(local_count, slot_rows, quarter)
    part_gate = jnp.einsum(
        "erd,edf->erf", routed_tokens, w_gate, preferred_element_type=jnp.float32
    )
    part_up = jnp.einsum("erd,edf->erf", routed_tokens, w_up, preferred_element_type=jnp.float32)
    routed_grads = routed_grads.reshape(local_count, slot_rows, quarter)
    part_back = jnp.einsum("erd,efd->erf", routed_grads, w_down, preferred_element_type=jnp.float32)
    weight = routed_weight.reshape(local_count, slot_rows).astype(jnp.float32)
    pre_gate, pre_up, pre_back = (
        lax.psum(part_gate.astype(jnp.bfloat16), "rep").astype(jnp.float32),
        lax.psum(part_up.astype(jnp.bfloat16), "rep").astype(jnp.float32),
        lax.psum(part_back.astype(jnp.bfloat16), "rep").astype(jnp.float32),
    )
    hidden, gate_delta, up_delta = hidden_terms(pre_gate, pre_up, pre_back, weight)
    scaled_grad = (weight[:, :, None] * routed_grads.astype(jnp.float32)).astype(jnp.bfloat16)
    back_rows = jnp.einsum("erf,edf->erd", gate_delta, w_gate, preferred_element_type=jnp.float32)
    back_rows = back_rows + jnp.einsum(
        "erf,edf->erd", up_delta, w_up, preferred_element_type=jnp.float32
    )
    back_rows = back_rows.astype(jnp.bfloat16).reshape(local_count, ep_ranks, CAP, quarter)
    returned = lax.all_to_all(back_rows, "ep", split_axis=1, concat_axis=1, tiled=True)
    grad_gate = jnp.einsum(
        "erd,erf->edf", routed_tokens, gate_delta, preferred_element_type=jnp.float32
    ).astype(jnp.bfloat16)
    grad_up = jnp.einsum(
        "erd,erf->edf", routed_tokens, up_delta, preferred_element_type=jnp.float32
    ).astype(jnp.bfloat16)
    grad_down = jnp.einsum(
        "erf,erd->efd", hidden, scaled_grad, preferred_element_type=jnp.float32
    ).astype(jnp.bfloat16)
    token_grad = jnp.einsum(
        "ts,sd->td",
        placing,
        returned.reshape(slot_total, quarter),
        preferred_element_type=jnp.float32,
    )
    return (token_grad.astype(jnp.bfloat16), grad_gate, grad_up, grad_down)


def solution(mesh):
    placed = (
        P("ep", "rep"),
        P("ep", "rep"),
        P("ep", None),
        P("ep", None),
        P("ep", "rep", None),
        P("ep", "rep", None),
        P("ep", None, "rep"),
    )
    return jax.shard_map(
        body,
        mesh=mesh,
        in_specs=placed,
        out_specs=(
            P("ep", "rep"),
            P("ep", "rep", None),
            P("ep", "rep", None),
            P("ep", None, "rep"),
        ),
        check_vma=False,
    )
```

profile of v0, /device:TPU:8, one launch (start us, length us, event | category | flops | bytes accessed | tf_op | source)
XLA Modules:
  0.0 345.2 jit_solution(13522083225533455690)
XLA Ops:
  7.2 0.0 copy-start
  7.2 0.9 copy.35
  8.0 0.2 convert_reduce_fusion
  8.3 0.2 reduce_window_sum.11
  8.4 2.4 select_reduce_fusion.1
  10.9 0.7 multiply_add_fusion
  11.6 0.1 copy.37
  11.7 0.6 copy-done.11
  12.3 1.5 fusion
  13.8 1.4 convolution_convert_fusion.3
  15.2 1.6 reshape.170
  16.8 17.5 %all-to-all-start.2 = ((bf16[1,128,9,512]{3,2,0,1:T(8,128)(2,1)}), bf16[1,128,9,512]{3,2,0,1:T(8,128)(2,1)S(1)}, u32[]{:S(2)}, u32[]{:S(2)}) async-start(bf16[1,128,9,512]{3,2,0,1:T(8,128)(2,1)} %bitcast.72), calls=%async_computation.2 | async-start | bytes 4194304 | tf_op jit(solution)/shard_map/all_to_all | solution.py:47
  34.3 1.5 convolution_convert_fusion.4
  35.8 3.3 reshape.167
  39.1 49.2 %all-to-all-done.2 = bf16[1,128,9,512]{3,2,0,1:T(8,128)(2,1)S(1)} async-done(((bf16[1,128,9,512]{3,2,0,1:T(8,128)(2,1)}), bf16[1,128,9,512]{3,2,0,1:T(8,128)(2,1)S(1)}, u32[]{:S(2)}, u32[]{:S(2)}) %all-to-all-start.2) | async-done | bytes 1179680 | tf_op jit(solution)/shard_map/all_to_all | solution.py:47
  88.4 1.3 copy-done.1
  89.7 6.1 %all-to-all-start.1 = ((bf16[1,128,9,512]{3,2,0,1:T(8,128)(2,1)}), bf16[1,128,9,512]{3,2,0,1:T(8,128)(2,1)S(1)}, u32[]{:S(2)}, u32[]{:S(2)}) async-start(bf16[1,128,9,512]{3,2,0,1:T(8,128)(2,1)} %bitcast.71), calls=%async_computation.1 | async-start | bytes 4194304 | tf_op jit(solution)/shard_map/all_to_all | solution.py:48
  95.7 0.0 copy-start.10
  95.7 0.2 all-reduce.3.cloned.1.call-start
  96.0 3.6 %reshape.171 = bf16[1152,512]{1,0:T(8,128)(2,1)} reshape(bf16[1,128,9,512]{3,2,0,1:T(8,128)(2,1)} %copy-done.1) | data formatting | bytes 2359296 | tf_op jit(solution)/shard_map/reshape.4
  99.6 3.6 %fusion.11 = bf16[1,1152,640]{2,1,0:T(8,128)(2,1)} fusion(bf16[1152,512]{1,0:T(8,128)(2,1)} %reshape.171, bf16[1,512,640]{2,1,0:T(8,128)(2,1)S(1)} %copy-done.10), kind=kOutput, calls=%fused_computation.26 | convolution fusion | flops 755712000 | bytes 3309568 | tf_op jit(solution)/shard_map/erd,edf->erf/dot_general | solution.py:55
  103.2 2.2 fusion.12
  105.4 44.4 %all-to-all-done.1 = bf16[1,128,9,512]{3,2,0,1:T(8,128)(2,1)S(1)} async-done(((bf16[1,128,9,512]{3,2,0,1:T(8,128)(2,1)}), bf16[1,128,9,512]{3,2,0,1:T(8,128)(2,1)S(1)}, u32[]{:S(2)}, u32[]{:S(2)}) %all-to-all-start.1) | async-done | bytes 1179680 | tf_op jit(solution)/shard_map/all_to_all | solution.py:48
  149.8 1.3 reshape.168
  151.1 3.7 %fusion.10 = bf16[1,1152,640]{2,1,0:T(8,128)(2,1)} fusion(bf16[1152,512]{1,0:T(8,128)(2,1)} %reshape.168, bf16[1,640,512]{2,1,0:T(8,128)(2,1)} %param.13), kind=kOutput, calls=%fused_computation.25 | convolution fusion | flops 755712000 | bytes 3309568 | tf_op jit(solution)/shard_map/erd,efd->erf/dot_general | solution.py:57
  154.9 0.0 all-reduce.3.cloned.1.call-update
  154.9 1.4 copy.38
  156.3 2.1 select_reduce_fusion
  158.4 1.6 convert_element_type.176
  159.9 16.8 %all_to_all.20 = bf16[1,128,9]{2,0,1:T(2,128)(2,1)S(1)} all-to-all(bf16[1,128,9]{2,0,1:T(2,128)(2,1)} %convert_element_type.176), channel_id=1, replica_groups=mesh['rep'=4,'ep'=128] {'ep'}, dimensions={1} | all-to-all | bytes 4608 | tf_op jit(solution)/shard_map/all_to_all | solution.py:49
  176.7 0.8 convert_reduce_fusion.1
  177.5 1.6 reshape.179
  179.2 76.7 %all-reduce.3.cloned.1.call-done = (bf16[1,1152,640]{2,1,0:T(8,128)(2,1)}, bf16[1,1152,640]{2,1,0:T(8,128)(2,1)}, bf16[1,1152,640]{2,1,0:T(8,128)(2,1)}) async-done(((bf16[1,1152,640]{2,1,0:T(8,128)(2,1)}, bf16[1,1152,640]{2,1,0:T(8,128)(2,1)}, bf16[1,1152,640]{2,1,0:T(8,128)(2,1)}), (bf16[1,1152,640]{2,1,0:T(8,128)(2,1)}, bf16[1,1152,640]{2,1,0:T(8,128)(2,1)}, ...) | async-done | bytes 4423696 | tf_op jit(solution)/shard_map/psum | solution.py:61
  255.9 3.5 %fusion.13 = (bf16[1152,640]{1,0:T(8,128)(2,1)S(1)}, bf16[1,1152,640]{2,1,0:T(8,128)(2,1)S(1)}) fusion(bf16[1,1152,640]{2,1,0:T(8,128)(2,1)} %get-tuple-element.6, f32[1152]{0:T(1024)} %reshape.179, bf16[1,1152,640]{2,1,0:T(8,128)(2,1)} %get-tuple-element.5, bf16[1,1152,640]{2,1,0:T(8,128)(2,1)} %get-tuple-element.4), kind=kLoop, calls=%fused_computation.29 | loop fusion | flops 12533760 | bytes 7377408 | tf_op jit(solution)/shard_map/reshape.25
  259.4 1.1 fusion.19
  260.5 0.4 copy-done.2
  260.9 2.2 fusion.1
  263.1 3.3 reshape.176
  266.4 14.6 %all-to-all-start.3 = ((bf16[1,128,9,512]{3,2,0,1:T(8,128)(2,1)}), bf16[1,128,9,512]{3,2,0,1:T(8,128)(2,1)}, u32[]{:S(2)}, u32[]{:S(2)}) async-start(bf16[1,128,9,512]{3,2,0,1:T(8,128)(2,1)} %bitcast.70), calls=%async_computation.3 | async-start | bytes 4194304 | tf_op jit(solution)/shard_map/all_to_all | solution.py:71
  281.1 0.0 copy-start.13
  281.1 4.2 %reshape.180 = f32[1,1152,1,1,1,1,512]{6,0,1,5,4,3,2:T(1,128)} reshape(bf16[1,128,9,512]{3,2,0,1:T(8,128)(2,1)S(1)} %all-to-all-done.1) | data formatting | bytes 3538944 | tf_op jit(solution)/shard_map/convert_element_type | solution.py:65
  285.3 5.4 %multiply_convert_fusion.1 = bf16[1,1152,1,1,1,1,512]{6,0,1,5,4,3,2:T(2,128)(2,1)S(1)} fusion(f32[1,1152,1,1,1,1,512]{6,0,1,5,4,3,2:T(1,128)} %reshape.180, f32[1152]{0:T(1024)S(1)} %copy-done.13), kind=kLoop, calls=%fused_computation.28 | loop fusion | flops 1179648 | bytes 3543552 | tf_op jit(solution)/shard_map/convert_element_type | solution.py:65
  290.7 2.0 fusion.27
  292.8 2.0 fusion.28
  294.8 2.2 fusion.31
  297.1 37.7 %all-to-all-done.3 = bf16[1,128,9,512]{3,2,0,1:T(8,128)(2,1)} async-done(((bf16[1,128,9,512]{3,2,0,1:T(8,128)(2,1)}), bf16[1,128,9,512]{3,2,0,1:T(8,128)(2,1)}, u32[]{:S(2)}, u32[]{:S(2)}) %all-to-all-start.3) | async-done | bytes 1179680 | tf_op jit(solution)/shard_map/all_to_all | solution.py:71
  334.8 2.5 reshape.177
  337.3 1.0 convolution_convert_fusion.6
  (24 shorter events, 0.1 us)
Async XLA Ops:
  7.2 96.0 %copy-start = (bf16[1,512,640]{2,1,0:T(8,128)(2,1)S(1)}, bf16[1,512,640]{2,1,0:T(8,128)(2,1)}, u32[]{:S(2)}) copy-start(bf16[1,512,640]{2,1,0:T(8,128)(2,1)} %param.11) | copy-start | bytes 1966084
  11.7 0.6 copy-start.11
  16.8 17.5 %copy-start.12 = (bf16[128,512]{1,0:T(8,128)(2,1)S(1)}, bf16[128,512]{1,0:T(8,128)(2,1)}, u32[]{:S(2)}) copy-start(bf16[128,512]{1,0:T(8,128)(2,1)} %param.8) | copy-start | bytes 393220
  16.8 71.6 %all-to-all-start.2 = ((bf16[1,128,9,512]{3,2,0,1:T(8,128)(2,1)}), bf16[1,128,9,512]{3,2,0,1:T(8,128)(2,1)S(1)}, u32[]{:S(2)}, u32[]{:S(2)}) async-start(bf16[1,128,9,512]{3,2,0,1:T(8,128)(2,1)} %bitcast.72), calls=%async_computation.2 | async-start | bytes 4194304 | tf_op jit(solution)/shard_map/all_to_all | solution.py:47
  88.4 1.3 copy-start.1
  89.7 60.1 %all-to-all-start.1 = ((bf16[1,128,9,512]{3,2,0,1:T(8,128)(2,1)}), bf16[1,128,9,512]{3,2,0,1:T(8,128)(2,1)S(1)}, u32[]{:S(2)}, u32[]{:S(2)}) async-start(bf16[1,128,9,512]{3,2,0,1:T(8,128)(2,1)} %bitcast.71), calls=%async_computation.1 | async-start | bytes 4194304 | tf_op jit(solution)/shard_map/all_to_all | solution.py:48
  95.7 3.8 %copy-start.10 = (bf16[1,512,640]{2,1,0:T(8,128)(2,1)S(1)}, bf16[1,512,640]{2,1,0:T(8,128)(2,1)}, u32[]{:S(2)}) copy-start(bf16[1,512,640]{2,1,0:T(8,128)(2,1)} %param.12) | copy-start | bytes 1966084
  95.7 160.1 %all-reduce.3.cloned.1.call-start = ((), (), s32[]{:S(2)}) async-start(), calls=%async_computation.4 | async-start | bytes 8847360 | tf_op jit(solution)/shard_map/psum | solution.py:61
  99.6 3.6 %copy-start.8 = (bf16[1152,512]{1,0:T(8,128)(2,1)S(1)}, bf16[1152,512]{1,0:T(8,128)(2,1)}, u32[]{:S(2)}) copy-start(bf16[1152,512]{1,0:T(8,128)(2,1)} %reshape.171) | copy-start | bytes 3538948
  259.4 1.1 copy-start.6
  259.4 1.6 copy-start.2
  266.4 68.3 %all-to-all-start.3 = ((bf16[1,128,9,512]{3,2,0,1:T(8,128)(2,1)}), bf16[1,128,9,512]{3,2,0,1:T(8,128)(2,1)}, u32[]{:S(2)}, u32[]{:S(2)}) async-start(bf16[1,128,9,512]{3,2,0,1:T(8,128)(2,1)} %bitcast.70), calls=%async_computation.3 | async-start | bytes 4194304 | tf_op jit(solution)/shard_map/all_to_all | solution.py:71
  281.1 4.3 %copy-start.13 = (f32[1152]{0:T(1024)S(1)}, f32[1152]{0:T(1024)}, u32[]{:S(2)}) copy-start(f32[1152]{0:T(1024)} %reshape.179) | copy-start | bytes 13828
  285.3 5.4 %copy-start.3 = (bf16[1152,640]{1,0:T(8,128)(2,1)S(1)}, bf16[1152,640]{1,0:T(8,128)(2,1)}, u32[]{:S(2)}) copy-start(bf16[1152,640]{1,0:T(8,128)(2,1)} %copy-done.2) | copy-start | bytes 4423684
  285.3 5.4 %copy-start.9 = (bf16[1152,512]{1,0:T(8,128)(2,1)S(1)}, bf16[1152,512]{1,0:T(8,128)(2,1)}, u32[]{:S(2)}) copy-start(bf16[1152,512]{1,0:T(8,128)(2,1)} %reshape.171) | copy-start | bytes 3538948
  290.7 2.1 copy-start.7
  292.8 2.1 copy-start.4
  292.8 2.1 copy-start.5
Sparse Core Ops, SparseCore 0:
  155.0 100.8 all-reduce.2
where the time goes:
time: 346 us; the launch traced here: 345 us
  waiting for transfers between devices  208 us (60%)
  starting transfers between devices  38.4 us (11%)
  local copies, waits for them, and re-layouts  27.9 us (8%)
  matrix products  23.1 us (7%)
  blocking collectives  16.8 us (5%)
  other arithmetic  16.7 us (5%)
  between operations  14.2 us (4%)
    psum x1, waiting for transfers between devices, body(): lax.psum(part_up.astype(jnp.bfloat16), 'rep').astype(jnp.float32)  76.7 us
    all_to_all x1, waiting for transfers between devices, body(): lax.all_to_all(send_tokens, 'ep', split_axis=1, concat_axis=1, tiled=True)  49.2 us
    all_to_all x1, waiting for transfers between devices, body(): lax.all_to_all(send_grads, 'ep', split_axis=1, concat_axis=1, tiled=True)  44.4 us
    all_to_all x1, waiting for transfers between devices, body(): lax.all_to_all(back_rows, 'ep', split_axis=1, concat_axis=1, tiled=True)  37.7 us
    all_to_all x1, starting transfers between devices, body(): lax.all_to_all(send_tokens, 'ep', split_axis=1, concat_axis=1, tiled=True)  17.5 us
    all_to_all x1, blocking collectives, body(): lax.all_to_all(send_weight, 'ep', split_axis=1, concat_axis=1, tiled=True)  16.8 us
    all_to_all x1, starting transfers between devices, body(): lax.all_to_all(back_rows, 'ep', split_axis=1, concat_axis=1, tiled=True)  14.6 us
  transfers between devices with their start and end apart: 4, of which 4 were waited for; matrix products, arithmetic and copies ran while one was open for 11% of the time, Pallas kernels for 0%

commit v1 on v0

--- a/solution.py
+++ b/solution.py
@@ -4,6 +4,12 @@
 from jax.sharding import PartitionSpec as P
 
 CAP = 9
+
+
+def summed_here(value, axis):
+    parts = lax.all_gather(value, axis, axis=0, tiled=False)
+    acc = parts.sum(axis=0)
+    return acc
 
 
 def hidden_terms(pre_gate, pre_up, pre_back, weight):
@@ -58,7 +64,7 @@
     weight = routed_weight.reshape(local_count, slot_rows).astype(jnp.float32)
     pre_gate, pre_up, pre_back = (
         lax.psum(part_gate.astype(jnp.bfloat16), "rep").astype(jnp.float32),
-        lax.psum(part_up.astype(jnp.bfloat16), "rep").astype(jnp.float32),
+        summed_here(part_up.astype(jnp.bfloat16), "rep").astype(jnp.float32),
         lax.psum(part_back.astype(jnp.bfloat16), "rep").astype(jnp.float32),
     )
     hidden, gate_delta, up_delta = hidden_terms(pre_gate, pre_up, pre_back, weight)

time: 346 us -> 332 us (0.960)
  blocking collectives: 16.8 us -> 148 us
  waiting for transfers between devices: 208 us -> 85.5 us
  starting transfers between devices: 38.4 us -> 14.7 us
  other arithmetic: 16.7 us -> 21.8 us
    all_to_all x0 -> x2, blocking collectives: none -> 131 us  [the longest x1 71.3 us: body(): lax.all_to_all(send_tokens, 'ep', split_axis=1, concat_axis=1, tiled=True)]
    all_to_all x2 -> x0, waiting for transfers between devices: 93.6 us -> none  [the longest x1 49.2 us: body(): lax.all_to_all(send_tokens, 'ep', split_axis=1, concat_axis=1, tiled=True)]
    psum x1, waiting for transfers between devices: 76.7 us -> 47.8 us  [body(): lax.psum(part_gate.astype(jnp.bfloat16), 'rep').astype(jnp.float32)]
    all_to_all x2 -> x0, starting transfers between devices: 23.6 us -> none  [the longest x1 17.5 us: body(): lax.all_to_all(send_tokens, 'ep', split_axis=1, concat_axis=1, tiled=True)]
    reduce_sum x0 -> x1, other arithmetic: none -> 5.12 us  [summed_here(): acc = parts.sum(axis=0)]
  transfers between devices with their start and end apart: 4 -> 3, of which waited for: 4 -> 2; matrix products, arithmetic and copies ran while one was open for 11% -> 11% of each run, Pallas kernels for 0% -> 0%
where the time goes in v1:
time: 332 us; the launch traced here: 331 us
  blocking collectives  148 us (45%)
  waiting for transfers between devices  85.5 us (26%)
  local copies, waits for them, and re-layouts  25.1 us (8%)
  other arithmetic  21.8 us (7%)
  matrix products  21.6 us (7%)
  starting transfers between devices  14.7 us (4%)
  between operations  14.2 us (4%)
    all_to_all x1, blocking collectives, body(): lax.all_to_all(send_tokens, 'ep', split_axis=1, concat_axis=1, tiled=True)  71.3 us
    all_to_all x1, blocking collectives, body(): lax.all_to_all(send_grads, 'ep', split_axis=1, concat_axis=1, tiled=True)  60.1 us
    psum x1, waiting for transfers between devices, body(): lax.psum(part_gate.astype(jnp.bfloat16), 'rep').astype(jnp.float32)  47.8 us
    all_to_all x1, waiting for transfers between devices, body(): lax.all_to_all(back_rows, 'ep', split_axis=1, concat_axis=1, tiled=True)  37.7 us
    all_to_all x1, blocking collectives, body(): lax.all_to_all(send_weight, 'ep', split_axis=1, concat_axis=1, tiled=True)  16.9 us
    all_to_all x1, starting transfers between devices, body(): lax.all_to_all(back_rows, 'ep', split_axis=1, concat_axis=1, tiled=True)  14.6 us
  transfers between devices with their start and end apart: 3, of which 2 were waited for; matrix products, arithmetic and copies ran while one was open for 11% of the time, Pallas kernels for 0%

profile of v1, /device:TPU:8, one launch (start us, length us, event | category | flops | bytes accessed | tf_op | source)
XLA Modules:
  0.0 331.3 jit_solution(11913290822685638270)
XLA Ops:
  7.2 0.0 copy-start
  7.2 0.0 all-gather.3.cloned.1.call-start
  7.2 0.8 copy.35
  8.1 0.2 convert_reduce_fusion
  8.3 0.2 reduce_window_sum.11
  8.5 2.4 select_reduce_fusion.1
  10.9 0.7 multiply_add_fusion
  11.6 0.1 copy.37
  11.7 1.5 fusion
  13.2 0.0 copy-done.11
  13.2 2.4 convolution_convert_fusion.3
  15.7 2.3 reshape.182
  18.0 71.3 %all_to_all.20 = bf16[1,128,9,512]{3,2,0,1:T(8,128)(2,1)} all-to-all(bf16[1,128,9,512]{3,2,0,1:T(8,128)(2,1)S(1)} %bitcast.81), channel_id=1, replica_groups=mesh['rep'=4,'ep'=128] {'ep'}, dimensions={1} | all-to-all | bytes 2359296 | tf_op jit(solution)/shard_map/all_to_all | solution.py:53
  89.3 2.6 reshape.183
  92.0 2.2 convolution_convert_fusion.1
  94.2 0.0 all-gather.3.cloned.1.call-update
  94.2 0.0 all-reduce.3.cloned.1.call-start
  94.2 0.8 copy-done.12
  95.1 0.5 convolution_convert_fusion.4
  95.6 1.6 reshape.179
  97.2 60.1 %all_to_all.21 = bf16[1,128,9,512]{3,2,0,1:T(8,128)(2,1)S(1)} all-to-all(bf16[1,128,9,512]{3,2,0,1:T(8,128)(2,1)} %bitcast.82), channel_id=1, replica_groups=mesh['rep'=4,'ep'=128] {'ep'}, dimensions={1} | all-to-all | bytes 2359296 | tf_op jit(solution)/shard_map/all_to_all | solution.py:54
  157.3 1.4 reshape.180
  158.6 3.6 %fusion.11 = bf16[1,1152,640]{2,1,0:T(8,128)(2,1)} fusion(bf16[1152,512]{1,0:T(8,128)(2,1)} %copy-done.7, bf16[1,512,640]{2,1,0:T(8,128)(2,1)S(1)} %copy-done), kind=kOutput, calls=%fused_computation.26 | convolution fusion | flops 755712000 | bytes 3309568 | tf_op jit(solution)/shard_map/erd,edf->erf/dot_general | solution.py:58
  162.3 2.3 fusion.10
  164.5 0.0 all-reduce.3.cloned.1.call-update
  164.5 1.4 copy.38
  166.0 2.1 select_reduce_fusion
  168.0 1.6 convert_element_type.188
  169.6 16.9 %all_to_all.22 = bf16[1,128,9]{2,0,1:T(2,128)(2,1)S(1)} all-to-all(bf16[1,128,9]{2,0,1:T(2,128)(2,1)} %convert_element_type.188), channel_id=1, replica_groups=mesh['rep'=4,'ep'=128] {'ep'}, dimensions={1} | all-to-all | bytes 4608 | tf_op jit(solution)/shard_map/all_to_all | solution.py:55
  186.5 0.8 convert_reduce_fusion.1
  187.3 1.6 reshape.191
  188.9 5.1 %reduce.2 = bf16[1152,640]{1,0:T(8,128)(2,1)} reduce(bf16[4,1152,640]{2,1,0:T(8,128)(2,1)} %bitcast.83, bf16[]{:T(256)} %constant.36.clone.1), dimensions={0}, to_apply=%region_6.7 | reduce | flops 2211840 | bytes 7372802 | tf_op jit(solution)/shard_map/reduce_sum | solution.py:11
  194.1 47.8 %all-reduce.3.cloned.1.call-done = (bf16[1,1152,640]{2,1,0:T(8,128)(2,1)}, bf16[1,1152,640]{2,1,0:T(8,128)(2,1)}) async-done(((bf16[1,1152,640]{2,1,0:T(8,128)(2,1)}, bf16[1,1152,640]{2,1,0:T(8,128)(2,1)}), (bf16[1,1152,640]{2,1,0:T(8,128)(2,1)}, bf16[1,1152,640]{2,1,0:T(8,128)(2,1)})) %all-reduce.3.cloned.1.call-update) | async-done | bytes 2949136 | tf_op jit(solution)/shard_map/psum | solution.py:66
  241.9 3.5 %fusion.12 = (bf16[1152,640]{1,0:T(8,128)(2,1)S(1)}, bf16[1,1152,640]{2,1,0:T(8,128)(2,1)S(1)}) fusion(bf16[1,1152,640]{2,1,0:T(8,128)(2,1)} %get-tuple-element.5, f32[1152]{0:T(1024)} %reshape.191, bf16[1,1152,640]{2,1,0:T(8,128)(2,1)} %get-tuple-element.4, bf16[1152,640]{1,0:T(8,128)(2,1)} %reduce.2), kind=kLoop, calls=%fused_computation.28 | loop fusion | flops 12533760 | bytes 7377408 | tf_op jit(solution)/shard_map/reshape.25
  245.4 1.1 fusion.19
  246.5 0.6 copy-done.1
  247.1 2.2 fusion.1
  249.3 3.3 reshape.188
  252.6 14.6 %all-to-all-start.3 = ((bf16[1,128,9,512]{3,2,0,1:T(8,128)(2,1)}), bf16[1,128,9,512]{3,2,0,1:T(8,128)(2,1)}, u32[]{:S(2)}, u32[]{:S(2)}) async-start(bf16[1,128,9,512]{3,2,0,1:T(8,128)(2,1)} %bitcast.80), calls=%async_computation.3 | async-start | bytes 4194304 | tf_op jit(solution)/shard_map/all_to_all | solution.py:77
  267.2 0.0 copy-start.13
  267.2 4.3 %reshape.193 = f32[1,1152,1,1,1,1,512]{6,0,1,5,4,3,2:T(1,128)} reshape(bf16[1,128,9,512]{3,2,0,1:T(8,128)(2,1)S(1)} %all_to_all.21) | data formatting | bytes 3538944 | tf_op jit(solution)/shard_map/convert_element_type | solution.py:71
  271.5 5.4 %multiply_convert_fusion.1 = bf16[1,1152,1,1,1,1,512]{6,0,1,5,4,3,2:T(2,128)(2,1)S(1)} fusion(f32[1,1152,1,1,1,1,512]{6,0,1,5,4,3,2:T(1,128)} %reshape.193, f32[1152]{0:T(1024)S(1)} %copy-done.13), kind=kLoop, calls=%fused_computation.27 | loop fusion | flops 1179648 | bytes 3543552 | tf_op jit(solution)/shard_map/convert_element_type | solution.py:71
  276.9 2.0 fusion.28
  279.0 2.0 fusion.27
  281.0 2.2 fusion.31
  283.2 37.7 %all-to-all-done.3 = bf16[1,128,9,512]{3,2,0,1:T(8,128)(2,1)} async-done(((bf16[1,128,9,512]{3,2,0,1:T(8,128)(2,1)}), bf16[1,128,9,512]{3,2,0,1:T(8,128)(2,1)}, u32[]{:S(2)}, u32[]{:S(2)}) %all-to-all-start.3) | async-done | bytes 1179680 | tf_op jit(solution)/shard_map/all_to_all | solution.py:77
  320.9 2.5 reshape.189
  323.4 1.0 convolution_convert_fusion.6
  (28 shorter events, 0.1 us)
Async XLA Ops:
  7.2 151.5 %copy-start = (bf16[1,512,640]{2,1,0:T(8,128)(2,1)S(1)}, bf16[1,512,640]{2,1,0:T(8,128)(2,1)}, u32[]{:S(2)}) copy-start(bf16[1,512,640]{2,1,0:T(8,128)(2,1)} %param.11) | copy-start | bytes 1966084
  7.2 181.8 %all-gather.3.cloned.1.call-start = ((), (), s32[]{:S(2)}) async-start(), calls=%async_computation.4 | async-start | bytes 7372800 | tf_op jit(solution)/shard_map/all_gather | solution.py:10
  11.7 1.5 copy-start.11
  89.3 2.6 copy-start.10
  92.0 2.2 copy-start.7
  94.2 0.9 copy-start.12
  94.2 147.7 %all-reduce.3.cloned.1.call-start = ((), (), s32[]{:S(2)}) async-start(), calls=%async_computation.5 | async-start | bytes 5898240 | tf_op jit(solution)/shard_map/psum | solution.py:66
  158.6 3.6 %copy-start.9 = (bf16[1152,512]{1,0:T(8,128)(2,1)S(1)}, bf16[1152,512]{1,0:T(8,128)(2,1)}, u32[]{:S(2)}) copy-start(bf16[1152,512]{1,0:T(8,128)(2,1)} %reshape.180) | copy-start | bytes 3538948
  158.6 3.6 %copy-start.14 = (bf16[1,640,512]{2,1,0:T(8,128)(2,1)S(1)}, bf16[1,640,512]{2,1,0:T(8,128)(2,1)}, u32[]{:S(2)}) copy-start(bf16[1,640,512]{2,1,0:T(8,128)(2,1)} %param.13) | copy-start | bytes 1966084
  245.4 1.1 copy-start.5
  245.4 1.7 copy-start.1
  252.6 68.3 %all-to-all-start.3 = ((bf16[1,128,9,512]{3,2,0,1:T(8,128)(2,1)}), bf16[1,128,9,512]{3,2,0,1:T(8,128)(2,1)}, u32[]{:S(2)}, u32[]{:S(2)}) async-start(bf16[1,128,9,512]{3,2,0,1:T(8,128)(2,1)} %bitcast.80), calls=%async_computation.3 | async-start | bytes 4194304 | tf_op jit(solution)/shard_map/all_to_all | solution.py:77
  267.2 4.3 %copy-start.13 = (f32[1152]{0:T(1024)S(1)}, f32[1152]{0:T(1024)}, u32[]{:S(2)}) copy-start(f32[1152]{0:T(1024)} %reshape.191) | copy-start | bytes 13828
  271.5 5.4 %copy-start.6 = (bf16[1,1152,640]{2,1,0:T(8,128)(2,1)S(1)}, bf16[1,1152,640]{2,1,0:T(8,128)(2,1)}, u32[]{:S(2)}) copy-start(bf16[1,1152,640]{2,1,0:T(8,128)(2,1)} %copy-done.5) | copy-start | bytes 4423684
  271.5 5.4 %copy-start.8 = (bf16[1152,512]{1,0:T(8,128)(2,1)S(1)}, bf16[1152,512]{1,0:T(8,128)(2,1)}, u32[]{:S(2)}) copy-start(bf16[1152,512]{1,0:T(8,128)(2,1)} %copy-done.7) | copy-start | bytes 3538948
  276.9 2.0 copy-start.2
  279.0 2.1 copy-start.3
  279.0 2.1 copy-start.4
Sparse Core Ops, SparseCore 0:
  94.3 61.0 all-gather.2
  164.7 77.1 all-reduce.2
